TPU v7x, 32 devices: a whole 2x2x4 slice. The times are simulated.
32 devices in a mesh: harm: 16 (over z, x, core), bus: 2 (over y).
Axes of the slice: x: 2, y: 2, z: 4, core: 2. Of those that a mesh axis runs over, the one named last changes fastest.
Arguments:
- conv_volt: bfloat16 [2, 64, 128, 128], P(None, None, ('bus', 'harm')), may hold values from -0.75 to 0.75
- conv_power: float32 [128, 128], P(('bus', 'harm')), may hold values from 0.2 to 2
- conv_type: int32 [128], P(('bus', 'harm')), may hold values from 0 to 7
- type_steep: float32 [8], replicated, may hold values from 0.5 to 4
- conv_bus: int32 [128], P(('bus', 'harm')), may hold values from 0 to 511, as said below
- admittance: float32 [2, 4, 64, 512], P(None, None, 'harm', 'bus'), may hold values from -0.5 to 1
- link_offset: int32 [3, 512], P(None, 'bus'), may hold values from -8 to 8, as said below
Outputs:
- bus_volt: bfloat16 [2, 64, 512, 128], P(None, 'harm', 'bus')
- conv_next: bfloat16 [2, 64, 128, 128], P(None, None, ('bus', 'harm'))
Inputs may be any that keep to these rules, and one draw needn't show every extreme that they name: `conv_bus`: converter c is attached to one of the buses from (c // 4) * 16 to (c // 4 + 1) * 16 - 1; a bus may carry several converters. `link_offset`: the first line of every bus spans exactly 8 buses, up or down; the others span 1 to 8 buses; no offset is zero.
All inputs are finite; a program needn't handle non-finite values.
Results may differ from a plain program's by a relative error of at most 0.0057.
Values may be sent and summed in bfloat16 or wider, within the bound.
A program may use at most 64 MiB of HBM per device.

v0:
```python
import math

import jax
import jax.numpy as jnp
from jax import lax
from jax.sharding import PartitionSpec as P

H = 64
NT = 1024
REACH = 8
ITERS = 3


def as_sent(array):
    return jax.tree.map(lambda a: a.astype(jnp.bfloat16) if a.dtype == jnp.float32 else a, array)


def extended_2(cells, sides, width):
    for axis, dim in sides:
        count = lax.axis_size(axis)
        ends = count - 1
        head = lax.slice_in_dim(cells, 0, width, axis=dim)
        tail = lax.slice_in_dim(cells, cells.shape[dim] - width, cells.shape[dim], axis=dim)
        cells = jnp.concatenate(
            [
                lax.ppermute(tail, axis, [(i, (i + 1) % count) for i in range(ends)]),
                cells,
                lax.ppermute(head, axis, [((i + 1) % count, i) for i in range(ends)]),
            ],
            axis=dim,
        )
    return cells


def make_basis():
    orders = jnp.arange(1, H + 1, dtype=jnp.int32)
    samples = jnp.arange(NT, dtype=jnp.int32)
    phases = (orders[:, None] * samples[None, :] % NT).astype(jnp.float32) * (2.0 * math.pi / NT)
    return jnp.concatenate([jnp.cos(phases), -jnp.sin(phases)], axis=0).astype(jnp.bfloat16)


def complex_product(left_real, left_imag, right_real, right_imag):
    return (
        left_real * right_real - left_imag * right_imag,
        left_real * right_imag + left_imag * right_real,
    )


def line_sum(inject_real, inject_imag, volt_real, volt_imag, lines_real, lines_imag, targets):
    total_real, total_imag = (inject_real, inject_imag)
    for line_num in range(targets.shape[0]):
        near_real = jnp.take(volt_real, targets[line_num], axis=1)
        near_imag = jnp.take(volt_imag, targets[line_num], axis=1)
        term_real, term_imag = complex_product(
            lines_real[line_num][:, :, None], lines_imag[line_num][:, :, None], near_real, near_imag
        )
        total_real = total_real + term_real
        total_imag = total_imag + term_imag
    return (total_real, total_imag)


def local(conv_volt, conv_power, conv_type, type_steep, conv_bus, admittance, link_offset):
    block_rows = admittance.shape[3]
    conv_count = conv_volt.shape[2]
    snapshots = conv_volt.shape[3]
    first_bus = lax.axis_index("bus") * block_rows
    harmonic_basis = make_basis()
    matches = conv_type[:, None] == jnp.arange(type_steep.shape[0], dtype=jnp.int32)[None, :]
    steepness = jnp.sum(jnp.where(matches, type_steep[None, :], 0.0), axis=1)
    volt_rows = conv_volt.reshape(2 * H, conv_count, snapshots)
    block_size = min(conv_count, 4)
    waveform = jnp.einsum(
        "kcs,kn->csn", volt_rows, harmonic_basis, preferred_element_type=jnp.float32
    )
    current = (
        conv_power[0:block_size, :, None] * jnp.tanh(steepness[0:block_size, None, None] * waveform)
    ).astype(jnp.bfloat16)
    spectra = jnp.einsum(
        "csn,kn->kcs", current, harmonic_basis, preferred_element_type=jnp.float32
    ) * NT ** (-0.5)
    pieces = spectra.astype(jnp.bfloat16)
    spectra = pieces.reshape(2, H, conv_count, snapshots)
    received = lax.all_to_all(spectra, "harm", split_axis=1, concat_axis=2, tiled=True)
    block_bus = lax.all_gather(conv_bus, "harm", axis=0, tiled=True) - first_bus
    summed = (
        jnp.zeros((2, received.shape[1], block_rows, snapshots), jnp.float32)
        .at[:, :, block_bus, :]
        .add(received.astype(jnp.float32))
    )
    injection = summed.astype(jnp.bfloat16)
    inject_real = injection[0].astype(jnp.float32)
    inject_imag = injection[1].astype(jnp.float32)
    inverse_real = admittance[0, 0][:, :, None]
    inverse_imag = admittance[1, 0][:, :, None]
    volt_real, volt_imag = complex_product(inverse_real, inverse_imag, inject_real, inject_imag)
    targets = jnp.arange(block_rows, dtype=jnp.int32)[None, :] + REACH + link_offset
    for sweep_index in range(ITERS - 1):
        extended = extended_2(as_sent(jnp.stack([volt_real, volt_imag])), (("bus", 2),), REACH)
        total_real, total_imag = line_sum(
            inject_real,
            inject_imag,
            extended[0],
            extended[1],
            admittance[0, 1:],
            admittance[1, 1:],
            targets,
        )
        volt_real, volt_imag = complex_product(inverse_real, inverse_imag, total_real, total_imag)
    bus_volt = jnp.stack([volt_real, volt_imag]).astype(jnp.bfloat16)
    picked = jnp.take(bus_volt, block_bus, axis=2)
    conv_next = lax.all_to_all(picked, "harm", split_axis=2, concat_axis=1, tiled=True)
    return (bus_volt, conv_next)


def solution(mesh):
    in_specs = (
        P(None, None, ("bus", "harm"), None),
        P(("bus", "harm"), None),
        P(("bus", "harm")),
        P(),
        P(("bus", "harm")),
        P(None, None, "harm", "bus"),
        P(None, "bus"),
    )
    out_specs = (P(None, "harm", "bus", None), P(None, None, ("bus", "harm"), None))
    return jax.shard_map(local, mesh=mesh, in_specs=in_specs, out_specs=out_specs, check_vma=False)
```

profile of v0, /device:TPU:0, one launch (start us, length us, event | category | flops | bytes accessed | tf_op | source)
XLA Modules:
  0.0 89.9 jit_solution(17024910230587955081)
XLA Ops:
  0.7 1.2 %cosine_convert_fusion = (bf16[64,1024]{1,0:T(8,128)(2,1)S(1)}, bf16[64,1024]{1,0:T(8,128)(2,1)S(1)}) fusion(s32[64]{0:T(128)S(1)} %iota_add_fusion.1), kind=kLoop, calls=%fused_computation.105 | loop fusion | flops 1114112 | bytes 262400 | tf_op jit(solution)/shard_map/convert.15
  1.9 0.9 select_reduce_fusion
  2.8 1.3 %fusion.3 = bf16[128,4,128]{2,0,1:T(8,128)(2,1)S(1)} fusion(f32[4]{0:T(128)S(1)} %select_reduce_fusion, f32[4,128]{1,0:T(4,128)} %param.10, bf16[64,1024]{1,0:T(8,128)(2,1)S(1)} %get-tuple-element.41, bf16[64,1024]{1,0:T(8,128)(2,1)S(1)} %get-tuple-element.40, bf16[128,4,128]{2,1,0:T(4,128)(2,1)S(1)} %bitcast.148), kind=kOutput, calls=%fused_computation.18 | convolution fusion | flops 271187968 | bytes 526352 | tf_op jit(solution)/shard_map/csn,kn->kcs/dot_general | solution.py:78
  4.1 0.8 copy.57
  4.9 7.4 %all-to-all-start = ((bf16[2,64,4,128]{3,0,2,1:T(2,128)(2,1)}), bf16[2,64,4,128]{3,0,2,1:T(2,128)(2,1)S(1)}, u32[]{:S(2)}, u32[]{:S(2)}) async-start(bf16[2,64,4,128]{3,0,2,1:T(2,128)(2,1)} %copy.57), calls=%async_computation | async-start | bytes 262144 | tf_op jit(solution)/shard_map/all_to_all | solution.py:83
  13.9 12.4 %all-reduce = s32[64]{0:T(128)S(1)} all-reduce(s32[64]{0:T(128)S(1)} %dynamic-update-slice), channel_id=1, replica_groups=mesh['harm'=16,'bus'=2] {'harm'}, use_global_device_ids=true, to_apply=%add | all-reduce | flops 64 | bytes 512
  27.1 3.5 %scatter_fusion = f32[2,4,256,128]{3,1,2,0:T(4,128)S(1)} fusion(f32[2,4,256,128]{3,1,2,0:T(4,128)S(1)} %broadcast_in_dim.45, s32[64]{0:T(128)S(1)} %get-tuple-element.12, f32[64,2,4,128]{3,2,1,0:T(4,128)S(1)} %bitcast.149), kind=kCustom, calls=%fused_computation.13 | custom fusion | flops 65536 | bytes 786688 | tf_op jit(solution)/shard_map/scatter-add | solution.py:88
  31.5 3.4 %collective-permute-start = (bf16[2,4,8,128]{3,1,2,0:T(4,128)(2,1)S(1)}, bf16[2,4,8,128]{3,1,2,0:T(4,128)(2,1)S(1)}, u32[]{:S(2)}, u32[]{:S(2)}) collective-permute-start(bf16[2,4,8,128]{3,1,2,0:T(4,128)(2,1)S(1)} %get-tuple-element.27), channel_id=1, source_target_pairs={{0,1},{2,3},{4,5},{6,7},{8,9},{10,11},{12,13},{14,15},{16,17},{18,... | collective-permute-start | bytes 49160 | tf_op jit(solution)/shard_map/ppermute | solution.py:26
  35.0 1.3 %collective-permute-start.1 = (bf16[2,4,8,128]{3,1,2,0:T(4,128)(2,1)S(1)}, bf16[2,4,8,128]{3,1,2,0:T(4,128)(2,1)S(1)}, u32[]{:S(2)}, u32[]{:S(2)}) collective-permute-start(bf16[2,4,8,128]{3,1,2,0:T(4,128)(2,1)S(1)} %get-tuple-element.28), channel_id=1, source_target_pairs={{1,0},{3,2},{5,4},{7,6},{9,8},{11,10},{13,12},{15,14},{17,16},{19,... | collective-permute-start | bytes 49160 | tf_op jit(solution)/shard_map/ppermute | solution.py:28
  37.2 3.4 %collective-permute-done.1 = bf16[2,4,8,128]{3,1,2,0:T(4,128)(2,1)S(1)} collective-permute-done((bf16[2,4,8,128]{3,1,2,0:T(4,128)(2,1)S(1)}, bf16[2,4,8,128]{3,1,2,0:T(4,128)(2,1)S(1)}, u32[]{:S(2)}, u32[]{:S(2)}) %collective-permute-start.1) | collective-permute-done | bytes 16416 | tf_op jit(solution)/shard_map/ppermute | solution.py:28
  41.3 1.0 %gather_fusion.1 = bf16[256,4,128]{2,1,0:T(4,128)(2,1)S(1)} fusion(bf16[4,272,128]{2,0,1:T(4,128)(2,1)S(1)} %get-tuple-element.24, s32[1024]{0:T(1024)S(1)} %pad_clamp_fusion.3), kind=kCustom, calls=%fused_computation.clone | custom fusion | bytes 525312 | tf_op jit(solution)/shard_map/jit(_take)/gather | solution.py:52
  42.3 1.0 %gather_fusion.2 = bf16[256,4,128]{2,1,0:T(4,128)(2,1)S(1)} fusion(bf16[4,272,128]{2,0,1:T(4,128)(2,1)S(1)} %get-tuple-element.23, s32[1024]{0:T(1024)S(1)} %pad_clamp_fusion.3), kind=kCustom, calls=%fused_computation.1.clone | custom fusion | bytes 525312 | tf_op jit(solution)/shard_map/jit(_take)/gather | solution.py:53
  43.3 1.0 %gather_fusion.3 = bf16[256,4,128]{2,1,0:T(4,128)(2,1)S(1)} fusion(bf16[4,272,128]{2,0,1:T(4,128)(2,1)S(1)} %get-tuple-element.24, s32[1024]{0:T(1024)S(1)} %pad_clamp_fusion.2), kind=kCustom, calls=%fused_computation.2.clone | custom fusion | bytes 525312 | tf_op jit(solution)/shard_map/jit(_take)/gather | solution.py:52
  44.2 1.0 %gather_fusion.4 = bf16[256,4,128]{2,1,0:T(4,128)(2,1)S(1)} fusion(bf16[4,272,128]{2,0,1:T(4,128)(2,1)S(1)} %get-tuple-element.23, s32[1024]{0:T(1024)S(1)} %pad_clamp_fusion.2), kind=kCustom, calls=%fused_computation.3.clone | custom fusion | bytes 525312 | tf_op jit(solution)/shard_map/jit(_take)/gather | solution.py:53
  45.2 1.7 %gather_fusion.5 = bf16[256,4,128]{2,1,0:T(4,128)(2,1)} fusion(bf16[4,272,128]{2,0,1:T(4,128)(2,1)S(1)} %get-tuple-element.24, s32[1024]{0:T(1024)S(1)} %pad_clamp_fusion.1), kind=kCustom, calls=%fused_computation.4.clone | custom fusion | bytes 525312 | tf_op jit(solution)/shard_map/jit(_take)/gather | solution.py:52
  46.9 1.7 %gather_fusion.6 = bf16[256,4,128]{2,1,0:T(4,128)(2,1)} fusion(bf16[4,272,128]{2,0,1:T(4,128)(2,1)S(1)} %get-tuple-element.23, s32[1024]{0:T(1024)S(1)} %pad_clamp_fusion.1), kind=kCustom, calls=%fused_computation.5.clone | custom fusion | bytes 525312 | tf_op jit(solution)/shard_map/jit(_take)/gather | solution.py:53
  48.6 5.4 %fusion.37 = (bf16[1,4,256,128]{3,1,2,0:T(4,128)(2,1)S(1)}, f32[4,256,128]{2,0,1:T(4,128)S(1)}, f32[4,256,128]{2,0,1:T(4,128)S(1)}) fusion(f32[4,256]{0,1:T(8,128)S(1)} %copy.61, f32[4,256]{0,1:T(8,128)S(1)} %copy.53, bf16[256,4,128]{2,1,0:T(4,128)(2,1)} %gather_fusion.5, f32[4,256]{0,1:T(8,128)S(1)} %copy.66, bf16[256,4,128]{2,1,0:T(4,128)(2,1)} %gather_fusion.6, ...), kind=kLoop, calls=%fused_computation.96 | loop fusion | flops 5505024 | bytes 3441408 | tf_op jit(solution)/shard_map/stack | solution.py:98
  54.6 1.6 %collective-permute-start.2 = (bf16[2,4,8,128]{3,1,2,0:T(4,128)(2,1)S(1)}, bf16[2,4,8,128]{3,1,2,0:T(4,128)(2,1)S(1)}, u32[]{:S(2)}, u32[]{:S(2)}) collective-permute-start(bf16[2,4,8,128]{3,1,2,0:T(4,128)(2,1)S(1)} %get-tuple-element.25), channel_id=1, source_target_pairs={{0,1},{2,3},{4,5},{6,7},{8,9},{10,11},{12,13},{14,15},{16,17},{18,... | collective-permute-start | bytes 49160 | tf_op jit(solution)/shard_map/ppermute | solution.py:26
  56.2 1.5 %collective-permute-start.3 = (bf16[2,4,8,128]{3,1,2,0:T(4,128)(2,1)S(1)}, bf16[2,4,8,128]{3,1,2,0:T(4,128)(2,1)S(1)}, u32[]{:S(2)}, u32[]{:S(2)}) collective-permute-start(bf16[2,4,8,128]{3,1,2,0:T(4,128)(2,1)S(1)} %get-tuple-element.26), channel_id=1, source_target_pairs={{1,0},{3,2},{5,4},{7,6},{9,8},{11,10},{13,12},{15,14},{17,16},{19,... | collective-permute-start | bytes 49160 | tf_op jit(solution)/shard_map/ppermute | solution.py:28
  57.7 4.1 %collective-permute-done.3 = bf16[2,4,8,128]{3,1,2,0:T(4,128)(2,1)S(1)} collective-permute-done((bf16[2,4,8,128]{3,1,2,0:T(4,128)(2,1)S(1)}, bf16[2,4,8,128]{3,1,2,0:T(4,128)(2,1)S(1)}, u32[]{:S(2)}, u32[]{:S(2)}) %collective-permute-start.3) | collective-permute-done | bytes 16416 | tf_op jit(solution)/shard_map/ppermute | solution.py:28
  62.6 1.0 %gather_fusion.7 = bf16[256,4,128]{2,1,0:T(4,128)(2,1)S(1)} fusion(bf16[4,272,128]{2,0,1:T(4,128)(2,1)S(1)} %get-tuple-element.22, s32[1024]{0:T(1024)S(1)} %pad_clamp_fusion.3), kind=kCustom, calls=%fused_computation.6.clone | custom fusion | bytes 525312 | tf_op jit(solution)/shard_map/jit(_take)/gather | solution.py:52
  63.5 1.0 %gather_fusion.9 = bf16[256,4,128]{2,1,0:T(4,128)(2,1)S(1)} fusion(bf16[4,272,128]{2,0,1:T(4,128)(2,1)S(1)} %get-tuple-element.22, s32[1024]{0:T(1024)S(1)} %pad_clamp_fusion.2), kind=kCustom, calls=%fused_computation.8.clone | custom fusion | bytes 525312 | tf_op jit(solution)/shard_map/jit(_take)/gather | solution.py:52
  64.5 1.0 %gather_fusion.8 = bf16[256,4,128]{2,1,0:T(4,128)(2,1)S(1)} fusion(bf16[4,272,128]{2,0,1:T(4,128)(2,1)S(1)} %get-tuple-element.21, s32[1024]{0:T(1024)S(1)} %pad_clamp_fusion.3), kind=kCustom, calls=%fused_computation.7.clone | custom fusion | bytes 525312 | tf_op jit(solution)/shard_map/jit(_take)/gather | solution.py:53
  65.5 1.0 %gather_fusion.10 = bf16[256,4,128]{2,1,0:T(4,128)(2,1)S(1)} fusion(bf16[4,272,128]{2,0,1:T(4,128)(2,1)S(1)} %get-tuple-element.21, s32[1024]{0:T(1024)S(1)} %pad_clamp_fusion.2), kind=kCustom, calls=%fused_computation.9.clone | custom fusion | bytes 525312 | tf_op jit(solution)/shard_map/jit(_take)/gather | solution.py:53
  66.5 1.7 %gather_fusion.12 = bf16[256,4,128]{2,1,0:T(4,128)(2,1)} fusion(bf16[4,272,128]{2,0,1:T(4,128)(2,1)S(1)} %get-tuple-element.21, s32[1024]{0:T(1024)S(1)} %pad_clamp_fusion.1), kind=kCustom, calls=%fused_computation.11.clone | custom fusion | bytes 525312 | tf_op jit(solution)/shard_map/jit(_take)/gather | solution.py:53
  68.2 1.7 %gather_fusion.11 = bf16[256,4,128]{2,1,0:T(4,128)(2,1)} fusion(bf16[4,272,128]{2,0,1:T(4,128)(2,1)S(1)} %get-tuple-element.22, s32[1024]{0:T(1024)S(1)} %pad_clamp_fusion.1), kind=kCustom, calls=%fused_computation.10.clone | custom fusion | bytes 525312 | tf_op jit(solution)/shard_map/jit(_take)/gather | solution.py:52
  69.8 5.4 %fusion.39 = (bf16[1,4,256,128]{3,1,2,0:T(4,128)(2,1)S(1)}, f32[4,256,128]{2,0,1:T(4,128)S(1)}, f32[4,256,128]{2,0,1:T(4,128)S(1)}) fusion(f32[4,256]{0,1:T(8,128)S(1)} %copy.61, f32[4,256]{0,1:T(8,128)S(1)} %copy.53, bf16[256,4,128]{2,1,0:T(4,128)(2,1)} %gather_fusion.11, f32[4,256]{0,1:T(8,128)S(1)} %copy.66, bf16[256,4,128]{2,1,0:T(4,128)(2,1)} %gather_fusion.12, ...), kind=kLoop, calls=%fused_computation.98 | loop fusion | flops 5505024 | bytes 3441408 | tf_op jit(solution)/shard_map/stack | solution.py:109
  76.2 0.7 gather_fusion
  76.9 0.8 select_bitcast_fusion
  77.8 3.5 %all-to-all-start.1 = ((bf16[2,4,64,128]{3,1,0,2:T(4,128)(2,1)}), bf16[2,4,64,128]{3,1,0,2:T(4,128)(2,1)S(1)}, u32[]{:S(2)}, u32[]{:S(2)}) async-start(bf16[2,4,64,128]{3,1,0,2:T(4,128)(2,1)} %select_bitcast_fusion), calls=%async_computation.1 | async-start | bytes 262144 | tf_op jit(solution)/shard_map/all_to_all | solution.py:111
  81.3 0.9 copy.69
  82.1 7.0 %all-to-all-done.1 = bf16[2,4,64,128]{3,1,0,2:T(4,128)(2,1)S(1)} async-done(((bf16[2,4,64,128]{3,1,0,2:T(4,128)(2,1)}), bf16[2,4,64,128]{3,1,0,2:T(4,128)(2,1)S(1)}, u32[]{:S(2)}, u32[]{:S(2)}) %all-to-all-start.1) | async-done | bytes 131104 | tf_op jit(solution)/shard_map/all_to_all | solution.py:111
  (54 shorter events, 7.0 us)
Async XLA Ops:
  0.6 2.1 %copy-start = (bf16[2,64,4,128]{3,2,1,0:T(4,128)(2,1)S(1)}, bf16[2,64,4,128]{3,2,1,0:T(4,128)(2,1)}, u32[]{:S(2)}) copy-start(bf16[2,64,4,128]{3,2,1,0:T(4,128)(2,1)} %param.9) | copy-start | bytes 393220
  2.8 9.6 %copy-start.2 = (s32[3,256]{1,0:T(4,128)S(1)}, s32[3,256]{1,0:T(4,128)}, u32[]{:S(2)}) copy-start(s32[3,256]{1,0:T(4,128)} %param.15) | copy-start | bytes 9220
  2.8 9.6 %copy-start.1 = (f32[2,4,4,256]{3,2,1,0:T(4,128)S(1)}, f32[2,4,4,256]{3,2,1,0:T(4,128)}, u32[]{:S(2)}) copy-start(f32[2,4,4,256]{3,2,1,0:T(4,128)} %param.14) | copy-start | bytes 98308
  2.8 9.7 %copy-start.4 = (u32[32]{0:T(128)S(1)}, u32[32]{0:T(128)}, u32[]{:S(2)}) copy-start(u32[32]{0:T(128)} %constant.65) | copy-start | bytes 388
  2.8 10.9 %copy-start.3 = (s32[4]{0:T(128)S(1)}, s32[4]{0:T(128)}, u32[]{:S(2)}) copy-start(s32[4]{0:T(128)} %param.13) | copy-start | bytes 52
  4.9 21.8 %all-to-all-start = ((bf16[2,64,4,128]{3,0,2,1:T(2,128)(2,1)}), bf16[2,64,4,128]{3,0,2,1:T(2,128)(2,1)S(1)}, u32[]{:S(2)}, u32[]{:S(2)}) async-start(bf16[2,64,4,128]{3,0,2,1:T(2,128)(2,1)} %copy.57), calls=%async_computation | async-start | bytes 262144 | tf_op jit(solution)/shard_map/all_to_all | solution.py:83
  31.5 5.6 %collective-permute-start = (bf16[2,4,8,128]{3,1,2,0:T(4,128)(2,1)S(1)}, bf16[2,4,8,128]{3,1,2,0:T(4,128)(2,1)S(1)}, u32[]{:S(2)}, u32[]{:S(2)}) collective-permute-start(bf16[2,4,8,128]{3,1,2,0:T(4,128)(2,1)S(1)} %get-tuple-element.27), channel_id=1, source_target_pairs={{0,1},{2,3},{4,5},{6,7},{8,9},{10,11},{12,13},{14,15},{16,17},{18,... | collective-permute-start | bytes 49160 | tf_op jit(solution)/shard_map/ppermute | solution.py:26
  35.0 5.6 %collective-permute-start.1 = (bf16[2,4,8,128]{3,1,2,0:T(4,128)(2,1)S(1)}, bf16[2,4,8,128]{3,1,2,0:T(4,128)(2,1)S(1)}, u32[]{:S(2)}, u32[]{:S(2)}) collective-permute-start(bf16[2,4,8,128]{3,1,2,0:T(4,128)(2,1)S(1)} %get-tuple-element.28), channel_id=1, source_target_pairs={{1,0},{3,2},{5,4},{7,6},{9,8},{11,10},{13,12},{15,14},{17,16},{19,... | collective-permute-start | bytes 49160 | tf_op jit(solution)/shard_map/ppermute | solution.py:28
  54.6 3.1 %collective-permute-start.2 = (bf16[2,4,8,128]{3,1,2,0:T(4,128)(2,1)S(1)}, bf16[2,4,8,128]{3,1,2,0:T(4,128)(2,1)S(1)}, u32[]{:S(2)}, u32[]{:S(2)}) collective-permute-start(bf16[2,4,8,128]{3,1,2,0:T(4,128)(2,1)S(1)} %get-tuple-element.25), channel_id=1, source_target_pairs={{0,1},{2,3},{4,5},{6,7},{8,9},{10,11},{12,13},{14,15},{16,17},{18,... | collective-permute-start | bytes 49160 | tf_op jit(solution)/shard_map/ppermute | solution.py:26
  56.2 5.6 %collective-permute-start.3 = (bf16[2,4,8,128]{3,1,2,0:T(4,128)(2,1)S(1)}, bf16[2,4,8,128]{3,1,2,0:T(4,128)(2,1)S(1)}, u32[]{:S(2)}, u32[]{:S(2)}) collective-permute-start(bf16[2,4,8,128]{3,1,2,0:T(4,128)(2,1)S(1)} %get-tuple-element.26), channel_id=1, source_target_pairs={{1,0},{3,2},{5,4},{7,6},{9,8},{11,10},{13,12},{15,14},{17,16},{19,... | collective-permute-start | bytes 49160 | tf_op jit(solution)/shard_map/ppermute | solution.py:28
  77.8 11.4 %all-to-all-start.1 = ((bf16[2,4,64,128]{3,1,0,2:T(4,128)(2,1)}), bf16[2,4,64,128]{3,1,0,2:T(4,128)(2,1)S(1)}, u32[]{:S(2)}, u32[]{:S(2)}) async-start(bf16[2,4,64,128]{3,1,0,2:T(4,128)(2,1)} %select_bitcast_fusion), calls=%async_computation.1 | async-start | bytes 262144 | tf_op jit(solution)/shard_map/all_to_all | solution.py:111
where the time goes:
time: 91.1 us; the launch traced here: 89.9 us
  other arithmetic  20.9 us (23%)
  local copies, waits for them, and re-layouts  20.1 us (22%)
  starting transfers between devices  18.7 us (21%)
  waiting for transfers between devices  14.6 us (16%)
  blocking collectives  12.4 us (14%)
  between operations  1.79 us (2%)
  matrix products  1.34 us (1%)
    unnamed x1, blocking collectives  12.4 us
    ppermute x2, waiting for transfers between devices, extended_2(): lax.ppermute(head, axis, [((i + 1) % count, i) for i in range(ends)])  7.56 us
    all_to_all x1, starting transfers between devices, local(): lax.all_to_all(spectra, 'harm', split_axis=1, concat_axis=2, tiled=True)  7.38 us
    gather x6, local copies, waits for them, and re-layouts, line_sum(): near_real = jnp.take(volt_real, targets[line_num], axis=1)  7.25 us
    gather x6, local copies, waits for them, and re-layouts, line_sum(): near_imag = jnp.take(volt_imag, targets[line_num], axis=1)  7.24 us
    all_to_all x1, waiting for transfers between devices, local(): lax.all_to_all(picked, 'harm', split_axis=2, concat_axis=1, tiled=True)  7.01 us
    another operation x3, other arithmetic, local(): bus_volt = jnp.stack([volt_real, volt_imag]).astype(jnp.bfloat16)  6.37 us
    another operation x2, other arithmetic, local(): jnp.stack([volt_real, volt_imag])  6 us
  transfers between devices with their start and end apart: 6, of which 3 were waited for; matrix products, arithmetic and copies ran while one was open for 3% of the time, Pallas kernels for 0%

commit v1 on v0

v1 whole, which is shorter than its diff:
```python
import functools
import math

import jax
import jax.numpy as jnp
import numpy as np
from jax import lax
from jax.experimental import pallas as pl
from jax.experimental.pallas import tpu as pltpu
from jax.sharding import PartitionSpec as P

NT = 1024
LANES = 128
CHUNKS = 4


def make_basis(orders):
    samples = np.arange(NT)
    phases = (np.arange(1, orders + 1)[:, None] * samples[None, :] % NT) * (2.0 * math.pi / NT)
    return np.concatenate([np.cos(phases), -np.sin(phases)], axis=0).astype(np.float32)


def kernel(
    nh,
    ny,
    near,
    volt_ref,
    power_ref,
    type_ref,
    steep_ref,
    bus_ref,
    adm_ref,
    off_ref,
    fwd_ref,
    inv_ref,
    perm_ref,
    back_ref,
    out_ref,
    next_ref,
    volts,
    send,
    recv,
    my_bus,
    buses,
    adm_side,
    off_side,
    weights,
    state,
    resp,
    send_back,
    result,
    spec_send,
    spec_recv,
    left_send,
    right_send,
    bus_send,
    bus_recv,
    bus_left,
    bus_right,
    side_send,
    side_recv,
    ret_send,
    ret_recv,
    local_sem,
    out_sem,
):
    me = lax.axis_index("harm")
    y = lax.axis_index("bus")
    hl = adm_ref.shape[2]
    block = adm_ref.shape[3]
    links = off_ref.shape[0]
    conv = power_ref.shape[0]
    sub = block // nh
    tiles = block // LANES + 1
    ext = tiles * LANES
    rows = 8 * (nh + 2)
    has_left = y > 0
    has_right = y < ny - 1

    barrier = pltpu.get_barrier_semaphore()

    def greet(d, by):
        pl.semaphore_signal(barrier, inc=1, device_id={"harm": d, "bus": by})

    def greet_peer(s, carry):
        greet(lax.rem(me + s, nh), y)
        return carry

    lax.fori_loop(1, nh, greet_peer, 0)

    @pl.when(has_left)
    def _():
        lax.fori_loop(0, nh, lambda d, c: (greet(d, y - 1), c)[1], 0)

    @pl.when(has_right)
    def _():
        lax.fori_loop(0, nh, lambda d, c: (greet(d, y + 1), c)[1], 0)

    span = volt_ref.shape[0] // conv
    per = LANES // conv
    for b in range(span // per):
        block_rows = jnp.dot(
            perm_ref[...], volt_ref[LANES * b : LANES * (b + 1), :], preferred_element_type=jnp.float32
        ).astype(jnp.bfloat16)
        for c in range(conv):
            volts[per * b : per * (b + 1), LANES * c : LANES * (c + 1)] = block_rows[per * c : per * (c + 1), :]
    steep = jnp.concatenate(
        [jnp.full((1, LANES), steep_ref[type_ref[c]], jnp.float32) for c in range(conv)], axis=1
    )
    power = jnp.concatenate([power_ref[c : c + 1, :] for c in range(conv)], axis=1) * NT ** (-0.5)
    part = NT // CHUNKS
    spectra = jnp.zeros((span, conv * LANES), jnp.float32)
    for q in range(CHUNKS):
        wave = jnp.dot(fwd_ref[part * q : part * (q + 1), :], volts[...], preferred_element_type=jnp.float32)
        now = jnp.tanh(steep * wave).astype(jnp.bfloat16)
        spectra = spectra + jnp.dot(
            inv_ref[:, part * q : part * (q + 1)], now, preferred_element_type=jnp.float32
        )
    spectra = (spectra * power).astype(jnp.bfloat16)
    per_dev = 8 * hl
    for b in range(span // per):
        stacked = jnp.concatenate(
            [spectra[per * b : per * (b + 1), LANES * c : LANES * (c + 1)] for c in range(conv)], axis=0
        )
        mixed = jnp.dot(back_ref[...], stacked, preferred_element_type=jnp.float32)
        count = LANES // per_dev
        send[count * b : count * (b + 1)] = mixed.reshape(count, hl, 8, LANES).astype(jnp.bfloat16)

    first = (y * nh + me) * sub
    row8 = lax.broadcasted_iota(jnp.int32, (8, LANES), 0) % conv
    numbers = jnp.zeros((8, LANES), jnp.float32)
    for c in range(conv):
        numbers = jnp.where(row8 == c, (bus_ref[c] - first).astype(jnp.float32), numbers)
    my_bus[...] = numbers.astype(jnp.bfloat16)

    @pl.when(jnp.logical_not(has_left))
    def _():
        recv[nh] = jnp.zeros(recv.shape[1:], recv.dtype)
        buses[nh] = jnp.zeros(buses.shape[1:], buses.dtype)
        adm_side[0] = jnp.zeros(adm_side.shape[1:], adm_side.dtype)
        off_side[0] = jnp.zeros(off_side.shape[1:], off_side.dtype)

    @pl.when(jnp.logical_not(has_right))
    def _():
        recv[nh + 1] = jnp.zeros(recv.shape[1:], recv.dtype)
        buses[nh + 1] = jnp.zeros(buses.shape[1:], buses.dtype)
        adm_side[1] = jnp.zeros(adm_side.shape[1:], adm_side.dtype)
        off_side[1] = jnp.zeros(off_side.shape[1:], off_side.dtype)

    pl.semaphore_wait(barrier, nh - 1 + nh * has_left.astype(jnp.int32) + nh * has_right.astype(jnp.int32))

    def remote(src, dst, send_sem, recv_sem, d, by):
        return pltpu.make_async_remote_copy(
            src_ref=src, dst_ref=dst, send_sem=send_sem, recv_sem=recv_sem, device_id={"harm": d, "bus": by}
        )

    def bus_copy(d, slot, by, sems):
        return remote(my_bus, buses.at[slot], sems.at[d], bus_recv.at[slot], d, by)

    def spec_copy(d, slot, by, sems):
        return remote(send.at[d], recv.at[slot], sems.at[d], spec_recv.at[slot], d, by)

    def ret_copy(d, source):
        place = next_ref.at[:, pl.ds(source * hl, hl)]
        return remote(send_back.at[d], place, ret_send.at[d], ret_recv.at[source], d, y)

    def side_copies(side):
        by = y + 1 if side == 0 else y - 1
        start = block - LANES if side == 0 else 0
        return (
            remote(
                adm_ref.at[:, :, :, pl.ds(start, LANES)],
                adm_side.at[side],
                side_send.at[side],
                side_recv.at[side],
                me,
                by,
            ),
            remote(
                off_ref.at[:, pl.ds(start, LANES)],
                off_side.at[side],
                side_send.at[2 + side],
                side_recv.at[2 + side],
                me,
                by,
            ),
        )

    send_right = jnp.logical_and(has_right, me == nh - 1)
    send_left = jnp.logical_and(has_left, me == 0)

    def each(low, body):
        def step(i, carry):
            body(i)
            return carry

        lax.fori_loop(low, nh, step, 0)

    def peer(s):
        return lax.rem(me + s, nh)

    each(1, lambda s: bus_copy(peer(s), me, y, bus_send).start())

    @pl.when(send_right)
    def _():
        each(0, lambda d: bus_copy(d, nh, y + 1, bus_right).start())

    @pl.when(send_left)
    def _():
        each(0, lambda d: bus_copy(d, nh + 1, y - 1, bus_left).start())

    @pl.when(has_right)
    def _():
        for copy in side_copies(0):
            copy.start()

    @pl.when(has_left)
    def _():
        for copy in side_copies(1):
            copy.start()

    each(1, lambda s: spec_copy(peer(s), me, y, spec_send).start())

    @pl.when(send_right)
    def _():
        each(0, lambda d: spec_copy(d, nh, y + 1, left_send).start())

    @pl.when(send_left)
    def _():
        each(0, lambda d: spec_copy(d, nh + 1, y - 1, right_send).start())

    recv[me] = send[me]
    buses[me] = my_bus[...]

    @pl.when(has_left)
    def _():
        for copy in side_copies(0):
            copy.wait_recv()

    @pl.when(has_right)
    def _():
        for copy in side_copies(1):
            copy.wait_recv()

    lane = lax.broadcasted_iota(jnp.int32, (1, LANES), 1)
    is_right = lane < LANES // 2

    def adm_row(p, k, h, t):
        if t < tiles - 1:
            return adm_ref[p, k, h : h + 1, LANES * t : LANES * (t + 1)]
        return jnp.where(is_right, adm_side[1, p, k, h : h + 1, :], adm_side[0, p, k, h : h + 1, :])

    def off_row(k, t):
        if t < tiles - 1:
            return off_ref[k : k + 1, LANES * t : LANES * (t + 1)]
        return jnp.where(is_right, off_side[1, k : k + 1, :], off_side[0, k : k + 1, :])

    low, high = LANES - 16, 2 * LANES + 16
    band = lax.broadcasted_iota(jnp.int32, (high - low, LANES), 0) + low
    for t in range(tiles):
        masks = [band == lane + LANES + off_row(k, t) for k in range(links)]
        for h in range(hl):
            d_real, d_imag = adm_row(0, 0, h, t), adm_row(1, 0, h, t)
            total_real = jnp.zeros(band.shape, jnp.float32)
            total_imag = jnp.zeros(band.shape, jnp.float32)
            for k in range(links):
                l_real, l_imag = adm_row(0, 1 + k, h, t), adm_row(1, 1 + k, h, t)
                total_real += jnp.where(masks[k], d_real * l_real - d_imag * l_imag, 0.0)
                total_imag += jnp.where(masks[k], d_real * l_imag + d_imag * l_real, 0.0)
            blank = jnp.zeros((low, 2 * LANES), jnp.bfloat16)
            weights[h, t, 0:low, :] = blank
            weights[h, t, high:, :] = blank
            weights[h, t, low:high, 0:LANES] = total_real.astype(jnp.bfloat16)
            weights[h, t, low:high, LANES:] = total_imag.astype(jnp.bfloat16)

    each(1, lambda s: bus_copy(peer(s), peer(s), y, bus_send).wait_recv())

    @pl.when(has_left)
    def _():
        bus_copy(0, nh, y, bus_send).wait_recv()

    @pl.when(has_right)
    def _():
        bus_copy(0, nh + 1, y, bus_send).wait_recv()

    row = lax.broadcasted_iota(jnp.int32, (rows, LANES), 0)
    slot = row // 8
    is_real = row % 8 < conv
    base = jnp.where(slot == nh, ext - sub, jnp.where(slot == nh + 1, block, slot * sub))
    at_bus = base + buses[...].astype(jnp.float32).reshape(rows, LANES).astype(jnp.int32)
    hits = [at_bus == lane + LANES * t for t in range(tiles)]
    own = 8 * nh
    pick_real = [
        jnp.where(jnp.logical_and(hits[t], is_real), 1.0, 0.0)[:own].astype(jnp.bfloat16) for t in range(tiles - 1)
    ]
    pick_imag = [
        jnp.where(jnp.logical_and(hits[t], jnp.logical_not(is_real)), 1.0, 0.0)[:own].astype(jnp.bfloat16)
        for t in range(tiles - 1)
    ]
    for h in range(hl):
        start_real, start_imag = [], []
        for t in range(tiles):
            d_real, d_imag = adm_row(0, 0, h, t), adm_row(1, 0, h, t)
            start_real.append(jnp.where(hits[t], jnp.where(is_real, d_real, -d_imag), 0.0))
            start_imag.append(jnp.where(hits[t], jnp.where(is_real, d_imag, d_real), 0.0))
        now_real, now_imag = start_real, start_imag
        for last in (False, True):
            for t in range(tiles):
                state[0:rows, LANES * t : LANES * (t + 1)] = now_real[t].astype(jnp.bfloat16)
                state[rows:, LANES * t : LANES * (t + 1)] = now_imag[t].astype(jnp.bfloat16)
            new_real, new_imag = [], []
            for t in range(tiles - 1 if last else tiles):
                around = jnp.concatenate(
                    [
                        state[:, LANES * j : LANES * (j + 1)]
                        for j in ((t - 1) % tiles, t, (t + 1) % tiles)
                    ],
                    axis=1,
                )
                both = jnp.dot(around, weights[h, t], preferred_element_type=jnp.float32)
                new_real.append(start_real[t] + both[:rows, :LANES] - both[rows:, LANES:])
                new_imag.append(start_imag[t] + both[:rows, LANES:] + both[rows:, :LANES])
            now_real, now_imag = new_real, new_imag
        chosen = jnp.zeros((own, rows), jnp.float32)
        for t in range(tiles - 1):
            real_t = now_real[t].T.astype(jnp.bfloat16)
            imag_t = now_imag[t].T.astype(jnp.bfloat16)
            resp[h, own + LANES * t : own + LANES * (t + 1), :] = real_t
            resp[h, own + block + LANES * t : own + block + LANES * (t + 1), :] = imag_t
            chosen += jnp.dot(pick_real[t], real_t, preferred_element_type=jnp.float32)
            chosen += jnp.dot(pick_imag[t], imag_t, preferred_element_type=jnp.float32)
        resp[h, 0:own, :] = chosen.astype(jnp.bfloat16)

    each(1, lambda s: spec_copy(peer(s), peer(s), y, spec_send).wait_recv())

    @pl.when(has_left)
    def _():
        spec_copy(0, nh, y, spec_send).wait_recv()

    @pl.when(has_right)
    def _():
        spec_copy(0, nh + 1, y, spec_send).wait_recv()

    arrived = []
    for h in range(hl):
        arrived.append(recv[:, h].astype(jnp.float32).reshape(rows, LANES).astype(jnp.bfloat16))
        at_conv = jnp.dot(resp[h, 0:own, :], arrived[h], preferred_element_type=jnp.float32)
        at_conv = at_conv.reshape(nh, 2, conv, LANES).astype(jnp.bfloat16)
        send_back[:, :, h] = at_conv
    each(1, lambda s: ret_copy(peer(s), me).start())
    keep = pltpu.make_async_copy(send_back.at[me], next_ref.at[:, pl.ds(me * hl, hl)], local_sem)
    keep.start()
    outs = []
    for h in range(hl):
        solved = jnp.dot(resp[h, own:, :], arrived[h], preferred_element_type=jnp.float32)
        result[:, h] = solved.astype(jnp.bfloat16).reshape(2, block, LANES)
        copy = pltpu.make_async_copy(result.at[:, h], out_ref.at[:, h], out_sem.at[h])
        copy.start()
        outs.append(copy)

    each(1, lambda s: bus_copy(peer(s), me, y, bus_send).wait_send())
    each(1, lambda s: spec_copy(peer(s), me, y, spec_send).wait_send())

    @pl.when(has_right)
    def _():
        for copy in side_copies(0):
            copy.wait_send()

    @pl.when(has_left)
    def _():
        for copy in side_copies(1):
            copy.wait_send()

    @pl.when(send_right)
    def _():
        each(0, lambda d: bus_copy(d, nh, y + 1, bus_right).wait_send())
        each(0, lambda d: spec_copy(d, nh, y + 1, left_send).wait_send())

    @pl.when(send_left)
    def _():
        each(0, lambda d: bus_copy(d, nh + 1, y - 1, bus_left).wait_send())
        each(0, lambda d: spec_copy(d, nh + 1, y - 1, right_send).wait_send())

    keep.wait()
    for copy in outs:
        copy.wait()
    each(1, lambda s: ret_copy(peer(s), me).wait_send())
    each(1, lambda s: ret_copy(peer(s), peer(s)).wait_recv())


def local(nh, ny, conv_volt, conv_power, conv_type, type_steep, conv_bus, admittance, link_offset):
    _, orders, conv, snaps = conv_volt.shape
    hl = orders // nh
    block = admittance.shape[3]
    tiles = block // LANES + 1
    rows = 8 * (nh + 2)
    span = 2 * orders
    basis = make_basis(orders)
    regrouped = basis.reshape(2, orders, NT).transpose(1, 0, 2).reshape(span, NT)
    per = LANES // conv
    perm = np.zeros((LANES, LANES), np.float32)
    for c in range(conv):
        for k in range(per):
            perm[per * c + k, conv * k + c] = 1.0
    vmem = pl.BlockSpec(memory_space=pltpu.VMEM)
    smem = pl.BlockSpec(memory_space=pltpu.SMEM)
    anywhere = pl.BlockSpec(memory_space=pl.ANY)
    bf16 = jnp.bfloat16
    dma = pltpu.SemaphoreType.DMA
    return pl.pallas_call(
        functools.partial(kernel, nh, ny, None),
        out_shape=(
            jax.ShapeDtypeStruct((2, hl, block, snaps), bf16),
            jax.ShapeDtypeStruct((2, orders, conv, snaps), bf16),
        ),
        in_specs=[vmem, vmem, smem, smem, smem, vmem, vmem, vmem, vmem, vmem, vmem],
        out_specs=(anywhere, anywhere),
        scratch_shapes=[
            pltpu.VMEM((span, conv * LANES), bf16),
            pltpu.VMEM((nh, hl, 8, LANES), bf16),
            pltpu.VMEM((nh + 2, hl, 8, LANES), bf16),
            pltpu.VMEM((8, LANES), bf16),
            pltpu.VMEM((nh + 2, 8, LANES), bf16),
            pltpu.VMEM((2,) + admittance.shape[:3] + (LANES,), jnp.float32),
            pltpu.VMEM((2, link_offset.shape[0], LANES), jnp.int32),
            pltpu.VMEM((hl, tiles, 3 * LANES, 2 * LANES), bf16),
            pltpu.VMEM((2 * rows, tiles * LANES), bf16),
            pltpu.VMEM((hl, 8 * nh + 2 * block, rows), bf16),
            pltpu.VMEM((nh, 2, hl, conv, LANES), bf16),
            pltpu.VMEM((2, hl, block, LANES), bf16),
            dma((nh,)),
            dma((nh + 2,)),
            dma((nh,)),
            dma((nh,)),
            dma((nh,)),
            dma((nh + 2,)),
            dma((nh,)),
            dma((nh,)),
            dma((4,)),
            dma((4,)),
            dma((nh,)),
            dma((nh,)),
            dma,
            dma((hl,)),
        ],
        compiler_params=pltpu.CompilerParams(collective_id=0, has_side_effects=True, vmem_limit_bytes=56 * 2**20),
        name="power_flow",
    )(
        conv_volt.reshape(span * conv, snaps),
        conv_power,
        conv_type,
        type_steep,
        conv_bus,
        admittance,
        link_offset,
        jnp.asarray(basis.T, bf16),
        jnp.asarray(regrouped, bf16),
        jnp.asarray(perm, bf16),
        jnp.asarray(perm.T, bf16),
    )


def solution(mesh):
    in_specs = (
        P(None, None, ("bus", "harm"), None),
        P(("bus", "harm"), None),
        P(("bus", "harm")),
        P(),
        P(("bus", "harm")),
        P(None, None, "harm", "bus"),
        P(None, "bus"),
    )
    out_specs = (P(None, "harm", "bus", None), P(None, None, ("bus", "harm"), None))
    body = functools.partial(local, mesh.shape["harm"], mesh.shape["bus"])
    return jax.shard_map(body, mesh=mesh, in_specs=in_specs, out_specs=out_specs, check_vma=False)
```

time: 91.1 us -> 26.8 us (0.29); the launches traced: 89.9 us -> 26.7 us
  Pallas kernels: 0 us -> 23.4 us
  other arithmetic: 20.9 us -> 0 us
  starting transfers between devices: 18.7 us -> 0 us
  local copies, waits for them, and re-layouts: 20.1 us -> 2.57 us
  waiting for transfers between devices: 14.6 us -> 0 us
  blocking collectives: 12.4 us -> 0 us
  matrix products: 1.34 us -> 0 us
  between operations: 1.79 us -> 0.65 us
    pallas_call x0 -> x1, Pallas kernels: none -> 23.4 us  [local(): pl.pallas_call(functools.partial(kernel, nh, ny, None), out_shape=(jax.Sh...]
    gather x13 -> x0, local copies, waits for them, and re-layouts: 15.2 us -> none  [the longest x6 7.25 us: line_sum(): near_real = jnp.take(volt_real, targets[line_num], axis=1)]
    another operation x7 -> x0, other arithmetic: 14.3 us -> none  [the longest x3 6.37 us: local(): bus_volt = jnp.stack([volt_real, volt_imag]).astype(jnp.bfloat16)]
    unnamed x1 -> x0, blocking collectives: 12.4 us -> none
    all_to_all x2 -> x0, starting transfers between devices: 10.9 us -> none  [the longest x1 7.38 us: local(): lax.all_to_all(spectra, 'harm', split_axis=1, concat_axis=2, tiled=True)]
    ppermute x4 -> x0, starting transfers between devices: 7.83 us -> none  [the longest x2 5.06 us: extended_2(): lax.ppermute(tail, axis, [(i, (i + 1) % count) for i in range(ends)])]
    ppermute x4 -> x0, waiting for transfers between devices: 7.57 us -> none  [the longest x2 7.56 us: extended_2(): lax.ppermute(head, axis, [((i + 1) % count, i) for i in range(ends)])]
    all_to_all x2 -> x0, waiting for transfers between devices: 7.01 us -> none  [the longest x1 7.01 us: local(): lax.all_to_all(picked, 'harm', split_axis=2, concat_axis=1, tiled=True)]
  transfers between devices with their start and end apart: 6 -> 0, of which waited for: 3 -> 0; matrix products, arithmetic and copies ran while one was open for 3% -> 0% of each run, Pallas kernels for 0% -> 0%
where the time goes in v1:
time: 26.8 us; the launch traced here: 26.7 us
  Pallas kernels  23.4 us (87%)
  local copies, waits for them, and re-layouts  2.57 us (10%)
  between operations  0.65 us (2%)
    pallas_call x1, Pallas kernels, local(): pl.pallas_call(functools.partial(kernel, nh, ny, None), out_shape=(jax.Sh...  23.4 us
    unnamed x4, local copies, waits for them, and re-layouts  2.57 us

profile of v1, /device:TPU:0, one launch (start us, length us, event | category | flops | bytes accessed | tf_op | source)
XLA Modules:
  0.0 26.7 jit_solution(2440445503620611903)
XLA Ops:
  0.6 23.4 %power_flow.1 = (bf16[2,4,256,128]{3,2,1,0:T(8,128)(2,1)}, bf16[2,64,4,128]{3,2,1,0:T(4,128)(2,1)}) custom-call(bf16[512,128]{1,0:T(8,128)(2,1)} %bitcast.1, f32[4,128]{1,0:T(4,128)} %power_ref.1, s32[4]{0:T(128)} %type_ref.1, f32[8]{0:T(128)} %steep_ref.1, s32[4]{0:T(128)} %bus_ref.1, f32[2,4,4,256]{3,2,1,0:T(4,128)} %adm_ref.1, s32[3,256]{1,0:T(4,128)} %off_ref.1, ...), custom_call_target="tpu_custom_call" | custom-call | tf_op jit(solution)/shard_map/power_flow/pallas_call | solution.py:410
  24.1 0.0 copy-start
  24.1 1.9 %copy.15 = bf16[2,4,256,128]{3,2,1,0:T(8,128)(2,1)} copy(bf16[2,4,256,128]{3,2,1,0:T(8,128)(2,1)} %get-tuple-element.4) | data formatting | bytes 1048576
  26.0 0.0 copy-done
  26.0 0.7 %copy.16 = bf16[2,64,4,128]{3,2,1,0:T(4,128)(2,1)} copy(bf16[2,64,4,128]{3,2,1,0:T(4,128)(2,1)S(1)} %copy-done) | data formatting | bytes 262144
Async XLA Ops:
  24.1 1.9 %copy-start = (bf16[2,64,4,128]{3,2,1,0:T(4,128)(2,1)S(1)}, bf16[2,64,4,128]{3,2,1,0:T(4,128)(2,1)}, u32[]{:S(2)}) copy-start(bf16[2,64,4,128]{3,2,1,0:T(4,128)(2,1)} %get-tuple-element.5) | copy-start | bytes 393220

commit v2 on v1

--- a/solution.py
+++ b/solution.py
@@ -23,7 +23,6 @@
 def kernel(
     nh,
     ny,
-    near,
     volt_ref,
     power_ref,
     type_ref,
@@ -48,7 +47,6 @@
     state,
     resp,
     send_back,
-    result,
     spec_send,
     spec_recv,
     left_send,
@@ -62,7 +60,6 @@
     ret_send,
     ret_recv,
     local_sem,
-    out_sem,
 ):
     me = lax.axis_index("harm")
     y = lax.axis_index("bus")
@@ -350,13 +347,9 @@
     each(1, lambda s: ret_copy(peer(s), me).start())
     keep = pltpu.make_async_copy(send_back.at[me], next_ref.at[:, pl.ds(me * hl, hl)], local_sem)
     keep.start()
-    outs = []
     for h in range(hl):
         solved = jnp.dot(resp[h, own:, :], arrived[h], preferred_element_type=jnp.float32)
-        result[:, h] = solved.astype(jnp.bfloat16).reshape(2, block, LANES)
-        copy = pltpu.make_async_copy(result.at[:, h], out_ref.at[:, h], out_sem.at[h])
-        copy.start()
-        outs.append(copy)
+        out_ref[:, h] = solved.astype(jnp.bfloat16).reshape(2, block, LANES)
 
     each(1, lambda s: bus_copy(peer(s), me, y, bus_send).wait_send())
     each(1, lambda s: spec_copy(peer(s), me, y, spec_send).wait_send())
@@ -382,10 +375,17 @@
         each(0, lambda d: spec_copy(d, nh + 1, y - 1, right_send).wait_send())
 
     keep.wait()
-    for copy in outs:
-        copy.wait()
     each(1, lambda s: ret_copy(peer(s), me).wait_send())
     each(1, lambda s: ret_copy(peer(s), peer(s)).wait_recv())
+
+
+def store(volt_ref, next_ref, volt_out, next_out, sems):
+    copies = [pltpu.make_async_copy(volt_ref.at[p], volt_out.at[p], sems.at[p]) for p in range(2)]
+    copies.append(pltpu.make_async_copy(next_ref, next_out, sems.at[2]))
+    for copy in copies:
+        copy.start()
+    for copy in copies:
+        copy.wait()
 
 
 def local(nh, ny, conv_volt, conv_power, conv_type, type_steep, conv_bus, admittance, link_offset):
@@ -407,14 +407,12 @@
     anywhere = pl.BlockSpec(memory_space=pl.ANY)
     bf16 = jnp.bfloat16
     dma = pltpu.SemaphoreType.DMA
-    return pl.pallas_call(
-        functools.partial(kernel, nh, ny, None),
-        out_shape=(
-            jax.ShapeDtypeStruct((2, hl, block, snaps), bf16),
-            jax.ShapeDtypeStruct((2, orders, conv, snaps), bf16),
-        ),
+    volt_shape, next_shape = (2, hl, block, snaps), (2, orders, conv, snaps)
+    solved = pl.pallas_call(
+        functools.partial(kernel, nh, ny),
+        out_shape=(pltpu.VMEM(volt_shape, bf16), pltpu.VMEM(next_shape, bf16)),
         in_specs=[vmem, vmem, smem, smem, smem, vmem, vmem, vmem, vmem, vmem, vmem],
-        out_specs=(anywhere, anywhere),
+        out_specs=(vmem, vmem),
         scratch_shapes=[
             pltpu.VMEM((span, conv * LANES), bf16),
             pltpu.VMEM((nh, hl, 8, LANES), bf16),
@@ -427,7 +425,6 @@
             pltpu.VMEM((2 * rows, tiles * LANES), bf16),
             pltpu.VMEM((hl, 8 * nh + 2 * block, rows), bf16),
             pltpu.VMEM((nh, 2, hl, conv, LANES), bf16),
-            pltpu.VMEM((2, hl, block, LANES), bf16),
             dma((nh,)),
             dma((nh + 2,)),
             dma((nh,)),
@@ -441,7 +438,6 @@
             dma((nh,)),
             dma((nh,)),
             dma,
-            dma((hl,)),
         ],
         compiler_params=pltpu.CompilerParams(collective_id=0, has_side_effects=True, vmem_limit_bytes=56 * 2**20),
         name="power_flow",
@@ -458,6 +454,15 @@
         jnp.asarray(perm, bf16),
         jnp.asarray(perm.T, bf16),
     )
+    return pl.pallas_call(
+        store,
+        out_shape=(jax.ShapeDtypeStruct(volt_shape, bf16), jax.ShapeDtypeStruct(next_shape, bf16)),
+        in_specs=[vmem, vmem],
+        out_specs=(anywhere, anywhere),
+        scratch_shapes=[dma((3,))],
+        compiler_params=pltpu.CompilerParams(vmem_limit_bytes=32 * 2**20),
+        name="store_results",
+    )(*solved)
 
 
 def solution(mesh):

time: 26.8 us -> 24.9 us (0.929)
  local copies, waits for them, and re-layouts: 2.57 us -> 0 us
  Pallas kernels: 23.4 us -> 24.2 us
    unnamed x4 -> x0, local copies, waits for them, and re-layouts: 2.57 us -> none
    pallas_call x1 -> x2, Pallas kernels: 23.4 us -> 24.2 us  [the longest x1 23.3 us: local(): pl.pallas_call(functools.partial(kernel, nh, ny), out_shape=(pltpu.VMEM(v...]
where the time goes in v2:
time: 24.9 us; the launch traced here: 24.8 us
  Pallas kernels  24.2 us (97%)
  between operations  0.64 us (3%)
    pallas_call x1, Pallas kernels, local(): pl.pallas_call(functools.partial(kernel, nh, ny), out_shape=(pltpu.VMEM(v...  23.3 us
    pallas_call x1, Pallas kernels, local(): pl.pallas_call(store, out_shape=(jax.ShapeDtypeStruct(volt_shape, bf16),...  0.86 us

profile of v2, /device:TPU:0, one launch (start us, length us, event | category | flops | bytes accessed | tf_op | source)
XLA Modules:
  0.0 24.8 jit_solution(162651397520839633)
XLA Ops:
  0.6 23.3 %power_flow.1 = (bf16[2,4,256,128]{3,2,1,0:T(8,128)(2,1)S(1)}, bf16[2,64,4,128]{3,2,1,0:T(4,128)(2,1)S(1)}) custom-call(bf16[512,128]{1,0:T(8,128)(2,1)} %bitcast.1, f32[4,128]{1,0:T(4,128)} %power_ref.1, s32[4]{0:T(128)} %type_ref.1, f32[8]{0:T(128)} %steep_ref.1, s32[4]{0:T(128)} %bus_ref.1, f32[2,4,4,256]{3,2,1,0:T(4,128)} %adm_ref.1, s32[3,256]{1,0:T(4,128)} %off_ref.1, ...), custom_call_target="tpu_custom_call" | custom-call | tf_op jit(solution)/shard_map/power_flow/pallas_call | solution.py:411
  23.9 0.9 %store_results.1 = (bf16[2,4,256,128]{3,2,1,0:T(8,128)(2,1)}, bf16[2,64,4,128]{3,2,1,0:T(4,128)(2,1)}) custom-call(bf16[2,4,256,128]{3,2,1,0:T(8,128)(2,1)S(1)} %get-tuple-element.4.volt_ref, bf16[2,64,4,128]{3,2,1,0:T(4,128)(2,1)S(1)} %get-tuple-element.5.next_ref), custom_call_target="tpu_custom_call" | custom-call | tf_op jit(solution)/shard_map/store_results/pallas_call | solution.py:457

commit v3 on v2

--- a/solution.py
+++ b/solution.py
@@ -44,7 +44,6 @@
     adm_side,
     off_side,
     weights,
-    state,
     resp,
     send_back,
     spec_send,
@@ -68,9 +67,9 @@
     links = off_ref.shape[0]
     conv = power_ref.shape[0]
     sub = block // nh
-    tiles = block // LANES + 1
-    ext = tiles * LANES
-    rows = 8 * (nh + 2)
+    tiles = block // LANES
+    around = LANES // sub
+    rows = 8 * (around + 2)
     has_left = y > 0
     has_right = y < ny - 1
 
@@ -132,8 +131,8 @@
 
     @pl.when(jnp.logical_not(has_left))
     def _():
-        recv[nh] = jnp.zeros(recv.shape[1:], recv.dtype)
-        buses[nh] = jnp.zeros(buses.shape[1:], buses.dtype)
+        recv[0] = jnp.zeros(recv.shape[1:], recv.dtype)
+        buses[0] = jnp.zeros(buses.shape[1:], buses.dtype)
         adm_side[0] = jnp.zeros(adm_side.shape[1:], adm_side.dtype)
         off_side[0] = jnp.zeros(off_side.shape[1:], off_side.dtype)
 
@@ -143,6 +142,54 @@
         buses[nh + 1] = jnp.zeros(buses.shape[1:], buses.dtype)
         adm_side[1] = jnp.zeros(adm_side.shape[1:], adm_side.dtype)
         off_side[1] = jnp.zeros(off_side.shape[1:], off_side.dtype)
+
+    lane = lax.broadcasted_iota(jnp.int32, (1, LANES), 1)
+    is_right = lane < LANES // 2
+
+    def adm_row(p, k, h, t, beyond):
+        def row_of(t):
+            if t < 0:
+                return adm_side[0, p, k, h : h + 1, :]
+            if t >= tiles:
+                return adm_side[1, p, k, h : h + 1, :]
+            return adm_ref[p, k, h : h + 1, LANES * t : LANES * (t + 1)]
+
+        return jnp.where(is_right, row_of(t + 1), row_of(t - 1)) if beyond else row_of(t)
+
+    def off_row(k, t, beyond):
+        def row_of(t):
+            if t < 0:
+                return off_side[0, k : k + 1, :]
+            if t >= tiles:
+                return off_side[1, k : k + 1, :]
+            return off_ref[k : k + 1, LANES * t : LANES * (t + 1)]
+
+        return jnp.where(is_right, row_of(t + 1), row_of(t - 1)) if beyond else row_of(t)
+
+    def fill(t, beyond, low, high):
+        band = lax.broadcasted_iota(jnp.int32, (high - low, LANES), 0) + low
+        shift = LANES if beyond else 0
+        masks = [
+            band == jnp.bitwise_and(lane + shift + off_row(k, t, beyond), 2 * LANES - 1) for k in range(links)
+        ]
+        at = 2 * shift
+        for h in range(hl):
+            d_real, d_imag = adm_row(0, 0, h, t, beyond), adm_row(1, 0, h, t, beyond)
+            total_real = jnp.zeros(band.shape, jnp.float32)
+            total_imag = jnp.zeros(band.shape, jnp.float32)
+            for k in range(links):
+                l_real, l_imag = adm_row(0, 1 + k, h, t, beyond), adm_row(1, 1 + k, h, t, beyond)
+                total_real += jnp.where(masks[k], d_real * l_real - d_imag * l_imag, 0.0)
+                total_imag += jnp.where(masks[k], d_real * l_imag + d_imag * l_real, 0.0)
+            weights[h, t, low:high, at : at + LANES] = total_real.astype(jnp.bfloat16)
+            weights[h, t, low:high, at + LANES : at + 2 * LANES] = total_imag.astype(jnp.bfloat16)
+
+    for t in range(tiles):
+        fill(t, False, 0, LANES + 16)
+        fill(t, False, 2 * LANES - 16, 2 * LANES)
+        for h in range(hl):
+            weights[h, t, LANES + 16 : 2 * LANES - 16, :] = jnp.zeros((LANES - 32, 4 * LANES), jnp.bfloat16)
+            weights[h, t, 16 : LANES - 16, 2 * LANES :] = jnp.zeros((LANES - 32, 2 * LANES), jnp.bfloat16)
 
     pl.semaphore_wait(barrier, nh - 1 + nh * has_left.astype(jnp.int32) + nh * has_right.astype(jnp.int32))
 
@@ -196,11 +243,11 @@
     def peer(s):
         return lax.rem(me + s, nh)
 
-    each(1, lambda s: bus_copy(peer(s), me, y, bus_send).start())
+    each(1, lambda s: bus_copy(peer(s), me + 1, y, bus_send).start())
 
     @pl.when(send_right)
     def _():
-        each(0, lambda d: bus_copy(d, nh, y + 1, bus_right).start())
+        each(0, lambda d: bus_copy(d, 0, y + 1, bus_right).start())
 
     @pl.when(send_left)
     def _():
@@ -216,18 +263,18 @@
         for copy in side_copies(1):
             copy.start()
 
-    each(1, lambda s: spec_copy(peer(s), me, y, spec_send).start())
+    each(1, lambda s: spec_copy(peer(s), me + 1, y, spec_send).start())
 
     @pl.when(send_right)
     def _():
-        each(0, lambda d: spec_copy(d, nh, y + 1, left_send).start())
+        each(0, lambda d: spec_copy(d, 0, y + 1, left_send).start())
 
     @pl.when(send_left)
     def _():
         each(0, lambda d: spec_copy(d, nh + 1, y - 1, right_send).start())
 
-    recv[me] = send[me]
-    buses[me] = my_bus[...]
+    recv[me + 1] = send[me]
+    buses[me + 1] = my_bus[...]
 
     @pl.when(has_left)
     def _():
@@ -239,120 +286,87 @@
         for copy in side_copies(1):
             copy.wait_recv()
 
-    lane = lax.broadcasted_iota(jnp.int32, (1, LANES), 1)
-    is_right = lane < LANES // 2
-
-    def adm_row(p, k, h, t):
-        if t < tiles - 1:
-            return adm_ref[p, k, h : h + 1, LANES * t : LANES * (t + 1)]
-        return jnp.where(is_right, adm_side[1, p, k, h : h + 1, :], adm_side[0, p, k, h : h + 1, :])
-
-    def off_row(k, t):
-        if t < tiles - 1:
-            return off_ref[k : k + 1, LANES * t : LANES * (t + 1)]
-        return jnp.where(is_right, off_side[1, k : k + 1, :], off_side[0, k : k + 1, :])
-
-    low, high = LANES - 16, 2 * LANES + 16
-    band = lax.broadcasted_iota(jnp.int32, (high - low, LANES), 0) + low
     for t in range(tiles):
-        masks = [band == lane + LANES + off_row(k, t) for k in range(links)]
+        for low, high in ((LANES - 16, LANES + 16), (2 * LANES - 16, 2 * LANES), (0, 16)):
+            fill(t, True, low, high)
+
+    each(1, lambda s: bus_copy(peer(s), peer(s) + 1, y, bus_send).wait_recv())
+
+    @pl.when(has_left)
+    def _():
+        bus_copy(0, 0, y, bus_send).wait_recv()
+
+    @pl.when(has_right)
+    def _():
+        bus_copy(0, nh + 1, y, bus_send).wait_recv()
+
+    row = lax.broadcasted_iota(jnp.int32, (rows, LANES), 0)
+    is_real = row % 8 < conv
+    base = jnp.bitwise_and((row // 8 - 1) * sub, 2 * LANES - 1)
+    own = 8 * around
+    for t in range(tiles):
+        near = buses[around * t : around * (t + 1) + 2].astype(jnp.float32).reshape(rows, LANES)
+        at_bus = base + near.astype(jnp.int32)
+        hits = [at_bus == lane, at_bus == lane + LANES]
+        picked = jnp.where(hits[0], 1.0, 0.0)
+        pick_real = jnp.where(is_real, picked, 0.0)[8 : 8 + own].astype(jnp.bfloat16)
+        pick_imag = jnp.where(is_real, 0.0, picked)[8 : 8 + own].astype(jnp.bfloat16)
         for h in range(hl):
-            d_real, d_imag = adm_row(0, 0, h, t), adm_row(1, 0, h, t)
-            total_real = jnp.zeros(band.shape, jnp.float32)
-            total_imag = jnp.zeros(band.shape, jnp.float32)
-            for k in range(links):
-                l_real, l_imag = adm_row(0, 1 + k, h, t), adm_row(1, 1 + k, h, t)
-                total_real += jnp.where(masks[k], d_real * l_real - d_imag * l_imag, 0.0)
-                total_imag += jnp.where(masks[k], d_real * l_imag + d_imag * l_real, 0.0)
-            blank = jnp.zeros((low, 2 * LANES), jnp.bfloat16)
-            weights[h, t, 0:low, :] = blank
-            weights[h, t, high:, :] = blank
-            weights[h, t, low:high, 0:LANES] = total_real.astype(jnp.bfloat16)
-            weights[h, t, low:high, LANES:] = total_imag.astype(jnp.bfloat16)
-
-    each(1, lambda s: bus_copy(peer(s), peer(s), y, bus_send).wait_recv())
-
-    @pl.when(has_left)
-    def _():
-        bus_copy(0, nh, y, bus_send).wait_recv()
-
-    @pl.when(has_right)
-    def _():
-        bus_copy(0, nh + 1, y, bus_send).wait_recv()
-
-    row = lax.broadcasted_iota(jnp.int32, (rows, LANES), 0)
-    slot = row // 8
-    is_real = row % 8 < conv
-    base = jnp.where(slot == nh, ext - sub, jnp.where(slot == nh + 1, block, slot * sub))
-    at_bus = base + buses[...].astype(jnp.float32).reshape(rows, LANES).astype(jnp.int32)
-    hits = [at_bus == lane + LANES * t for t in range(tiles)]
-    own = 8 * nh
-    pick_real = [
-        jnp.where(jnp.logical_and(hits[t], is_real), 1.0, 0.0)[:own].astype(jnp.bfloat16) for t in range(tiles - 1)
-    ]
-    pick_imag = [
-        jnp.where(jnp.logical_and(hits[t], jnp.logical_not(is_real)), 1.0, 0.0)[:own].astype(jnp.bfloat16)
-        for t in range(tiles - 1)
-    ]
-    for h in range(hl):
-        start_real, start_imag = [], []
-        for t in range(tiles):
-            d_real, d_imag = adm_row(0, 0, h, t), adm_row(1, 0, h, t)
-            start_real.append(jnp.where(hits[t], jnp.where(is_real, d_real, -d_imag), 0.0))
-            start_imag.append(jnp.where(hits[t], jnp.where(is_real, d_imag, d_real), 0.0))
-        now_real, now_imag = start_real, start_imag
-        for last in (False, True):
-            for t in range(tiles):
-                state[0:rows, LANES * t : LANES * (t + 1)] = now_real[t].astype(jnp.bfloat16)
-                state[rows:, LANES * t : LANES * (t + 1)] = now_imag[t].astype(jnp.bfloat16)
-            new_real, new_imag = [], []
-            for t in range(tiles - 1 if last else tiles):
-                around = jnp.concatenate(
-                    [
-                        state[:, LANES * j : LANES * (j + 1)]
-                        for j in ((t - 1) % tiles, t, (t + 1) % tiles)
-                    ],
-                    axis=1,
-                )
-                both = jnp.dot(around, weights[h, t], preferred_element_type=jnp.float32)
-                new_real.append(start_real[t] + both[:rows, :LANES] - both[rows:, LANES:])
-                new_imag.append(start_imag[t] + both[:rows, LANES:] + both[rows:, :LANES])
-            now_real, now_imag = new_real, new_imag
-        chosen = jnp.zeros((own, rows), jnp.float32)
-        for t in range(tiles - 1):
-            real_t = now_real[t].T.astype(jnp.bfloat16)
-            imag_t = now_imag[t].T.astype(jnp.bfloat16)
-            resp[h, own + LANES * t : own + LANES * (t + 1), :] = real_t
-            resp[h, own + block + LANES * t : own + block + LANES * (t + 1), :] = imag_t
-            chosen += jnp.dot(pick_real[t], real_t, preferred_element_type=jnp.float32)
-            chosen += jnp.dot(pick_imag[t], imag_t, preferred_element_type=jnp.float32)
-        resp[h, 0:own, :] = chosen.astype(jnp.bfloat16)
-
-    each(1, lambda s: spec_copy(peer(s), peer(s), y, spec_send).wait_recv())
-
-    @pl.when(has_left)
-    def _():
-        spec_copy(0, nh, y, spec_send).wait_recv()
+            start_real, start_imag = [], []
+            for side in (False, True):
+                d_real, d_imag = adm_row(0, 0, h, t, side), adm_row(1, 0, h, t, side)
+                start_real.append(jnp.where(hits[side], jnp.where(is_real, d_real, -d_imag), 0.0))
+                start_imag.append(jnp.where(hits[side], jnp.where(is_real, d_imag, d_real), 0.0))
+            now_real, now_imag = start_real, start_imag
+            for last in (False, True):
+                state = jnp.concatenate(
+                    [jnp.concatenate(now_real, axis=1), jnp.concatenate(now_imag, axis=1)], axis=0
+                ).astype(jnp.bfloat16)
+                width = 2 * LANES if last else 4 * LANES
+                both = jnp.dot(state, weights[h, t, :, 0:width], preferred_element_type=jnp.float32)
+                new_real, new_imag = [], []
+                for a in range(1 if last else 2):
+                    at = 2 * LANES * a
+                    left, right = both[:, at : at + LANES], both[:, at + LANES : at + 2 * LANES]
+                    new_real.append(start_real[a] + left[:rows] - right[rows:])
+                    new_imag.append(start_imag[a] + right[:rows] + left[rows:])
+                now_real, now_imag = new_real, new_imag
+            real_t = now_real[0].T.astype(jnp.bfloat16)
+            imag_t = now_imag[0].T.astype(jnp.bfloat16)
+            resp[h, t, own : own + LANES, :] = real_t
+            resp[h, t, own + LANES :, :] = imag_t
+            chosen = jnp.dot(pick_real, real_t, preferred_element_type=jnp.float32)
+            chosen += jnp.dot(pick_imag, imag_t, preferred_element_type=jnp.float32)
+            resp[h, t, 0:own, :] = chosen.astype(jnp.bfloat16)
+
+    each(1, lambda s: spec_copy(peer(s), peer(s) + 1, y, spec_send).wait_recv())
+
+    @pl.when(has_left)
+    def _():
+        spec_copy(0, 0, y, spec_send).wait_recv()
 
     @pl.when(has_right)
     def _():
         spec_copy(0, nh + 1, y, spec_send).wait_recv()
 
     arrived = []
-    for h in range(hl):
-        arrived.append(recv[:, h].astype(jnp.float32).reshape(rows, LANES).astype(jnp.bfloat16))
-        at_conv = jnp.dot(resp[h, 0:own, :], arrived[h], preferred_element_type=jnp.float32)
-        at_conv = at_conv.reshape(nh, 2, conv, LANES).astype(jnp.bfloat16)
-        send_back[:, :, h] = at_conv
+    for t in range(tiles):
+        for h in range(hl):
+            here = recv[around * t : around * (t + 1) + 2, h].astype(jnp.float32)
+            arrived.append(here.reshape(rows, LANES).astype(jnp.bfloat16))
+            at_conv = jnp.dot(resp[h, t, 0:own, :], arrived[-1], preferred_element_type=jnp.float32)
+            at_conv = at_conv.reshape(around, 2, conv, LANES).astype(jnp.bfloat16)
+            send_back[around * t : around * (t + 1), :, h] = at_conv
     each(1, lambda s: ret_copy(peer(s), me).start())
     keep = pltpu.make_async_copy(send_back.at[me], next_ref.at[:, pl.ds(me * hl, hl)], local_sem)
     keep.start()
-    for h in range(hl):
-        solved = jnp.dot(resp[h, own:, :], arrived[h], preferred_element_type=jnp.float32)
-        out_ref[:, h] = solved.astype(jnp.bfloat16).reshape(2, block, LANES)
-
-    each(1, lambda s: bus_copy(peer(s), me, y, bus_send).wait_send())
-    each(1, lambda s: spec_copy(peer(s), me, y, spec_send).wait_send())
+    for t in range(tiles):
+        for h in range(hl):
+            solved = jnp.dot(resp[h, t, own:, :], arrived[t * hl + h], preferred_element_type=jnp.float32)
+            out_ref[:, h, LANES * t : LANES * (t + 1)] = solved.astype(jnp.bfloat16).reshape(2, LANES, LANES)
+
+    each(1, lambda s: bus_copy(peer(s), me + 1, y, bus_send).wait_send())
+    each(1, lambda s: spec_copy(peer(s), me + 1, y, spec_send).wait_send())
 
     @pl.when(has_right)
     def _():
@@ -366,8 +380,8 @@
 
     @pl.when(send_right)
     def _():
-        each(0, lambda d: bus_copy(d, nh, y + 1, bus_right).wait_send())
-        each(0, lambda d: spec_copy(d, nh, y + 1, left_send).wait_send())
+        each(0, lambda d: bus_copy(d, 0, y + 1, bus_right).wait_send())
+        each(0, lambda d: spec_copy(d, 0, y + 1, left_send).wait_send())
 
     @pl.when(send_left)
     def _():
@@ -392,8 +406,9 @@
     _, orders, conv, snaps = conv_volt.shape
     hl = orders // nh
     block = admittance.shape[3]
-    tiles = block // LANES + 1
-    rows = 8 * (nh + 2)
+    tiles = block // LANES
+    around = LANES * nh // block
+    rows = 8 * (around + 2)
     span = 2 * orders
     basis = make_basis(orders)
     regrouped = basis.reshape(2, orders, NT).transpose(1, 0, 2).reshape(span, NT)
@@ -421,9 +436,8 @@
             pltpu.VMEM((nh + 2, 8, LANES), bf16),
             pltpu.VMEM((2,) + admittance.shape[:3] + (LANES,), jnp.float32),
             pltpu.VMEM((2, link_offset.shape[0], LANES), jnp.int32),
-            pltpu.VMEM((hl, tiles, 3 * LANES, 2 * LANES), bf16),
-            pltpu.VMEM((2 * rows, tiles * LANES), bf16),
-            pltpu.VMEM((hl, 8 * nh + 2 * block, rows), bf16),
+            pltpu.VMEM((hl, tiles, 2 * LANES, 4 * LANES), bf16),
+            pltpu.VMEM((hl, tiles, 8 * around + 2 * LANES, rows), bf16),
             pltpu.VMEM((nh, 2, hl, conv, LANES), bf16),
             dma((nh,)),
             dma((nh + 2,)),

time: 24.9 us -> 24.1 us (0.968)
  Pallas kernels: 24.2 us -> 23.3 us
    pallas_call x1, Pallas kernels: 23.3 us -> 22.5 us  [local(): pl.pallas_call(functools.partial(kernel, nh, ny), out_shape=(pltpu.VMEM(v...]
where the time goes in v3:
time: 24.1 us; the launch traced here: 24 us
  Pallas kernels  23.3 us (97%)
  between operations  0.64 us (3%)
    pallas_call x1, Pallas kernels, local(): pl.pallas_call(functools.partial(kernel, nh, ny), out_shape=(pltpu.VMEM(v...  22.5 us
    pallas_call x1, Pallas kernels, local(): pl.pallas_call(store, out_shape=(jax.ShapeDtypeStruct(volt_shape, bf16),...  0.86 us

profile of v3, /device:TPU:0, one launch (start us, length us, event | category | flops | bytes accessed | tf_op | source)
XLA Modules:
  0.0 24.0 jit_solution(14004298907745848791)
XLA Ops:
  0.6 22.5 %power_flow.1 = (bf16[2,4,256,128]{3,2,1,0:T(8,128)(2,1)S(1)}, bf16[2,64,4,128]{3,2,1,0:T(4,128)(2,1)S(1)}) custom-call(bf16[512,128]{1,0:T(8,128)(2,1)} %bitcast.1, f32[4,128]{1,0:T(4,128)} %power_ref.1, s32[4]{0:T(128)} %type_ref.1, f32[8]{0:T(128)} %steep_ref.1, s32[4]{0:T(128)} %bus_ref.1, f32[2,4,4,256]{3,2,1,0:T(4,128)} %adm_ref.1, s32[3,256]{1,0:T(4,128)} %off_ref.1, ...), custom_call_target="tpu_custom_call" | custom-call | tf_op jit(solution)/shard_map/power_flow/pallas_call | solution.py:426
  23.1 0.9 %store_results.1 = (bf16[2,4,256,128]{3,2,1,0:T(8,128)(2,1)}, bf16[2,64,4,128]{3,2,1,0:T(4,128)(2,1)}) custom-call(bf16[2,4,256,128]{3,2,1,0:T(8,128)(2,1)S(1)} %get-tuple-element.4.volt_ref, bf16[2,64,4,128]{3,2,1,0:T(4,128)(2,1)S(1)} %get-tuple-element.5.next_ref), custom_call_target="tpu_custom_call" | custom-call | tf_op jit(solution)/shard_map/store_results/pallas_call | solution.py:471

commit v4 on v3

--- a/solution.py
+++ b/solution.py
@@ -92,6 +92,147 @@
     def _():
         lax.fori_loop(0, nh, lambda d, c: (greet(d, y + 1), c)[1], 0)
 
+    first = (y * nh + me) * sub
+    row8 = lax.broadcasted_iota(jnp.int32, (8, LANES), 0) % conv
+    numbers = jnp.zeros((8, LANES), jnp.float32)
+    for c in range(conv):
+        numbers = jnp.where(row8 == c, (bus_ref[c] - first).astype(jnp.float32), numbers)
+    my_bus[...] = numbers.astype(jnp.bfloat16)
+
+    @pl.when(jnp.logical_not(has_left))
+    def _():
+        recv[0] = jnp.zeros(recv.shape[1:], recv.dtype)
+        buses[0] = jnp.zeros(buses.shape[1:], buses.dtype)
+        adm_side[0] = jnp.zeros(adm_side.shape[1:], adm_side.dtype)
+        off_side[0] = jnp.zeros(off_side.shape[1:], off_side.dtype)
+
+    @pl.when(jnp.logical_not(has_right))
+    def _():
+        recv[nh + 1] = jnp.zeros(recv.shape[1:], recv.dtype)
+        buses[nh + 1] = jnp.zeros(buses.shape[1:], buses.dtype)
+        adm_side[1] = jnp.zeros(adm_side.shape[1:], adm_side.dtype)
+        off_side[1] = jnp.zeros(off_side.shape[1:], off_side.dtype)
+
+    lane = lax.broadcasted_iota(jnp.int32, (1, LANES), 1)
+    is_right = lane < LANES // 2
+
+    def adm_row(p, k, h, t, beyond):
+        def row_of(t):
+            if t < 0:
+                return adm_side[0, p, k, h : h + 1, :]
+            if t >= tiles:
+                return adm_side[1, p, k, h : h + 1, :]
+            return adm_ref[p, k, h : h + 1, LANES * t : LANES * (t + 1)]
+
+        return jnp.where(is_right, row_of(t + 1), row_of(t - 1)) if beyond else row_of(t)
+
+    def off_row(k, t, beyond):
+        def row_of(t):
+            if t < 0:
+                return off_side[0, k : k + 1, :]
+            if t >= tiles:
+                return off_side[1, k : k + 1, :]
+            return off_ref[k : k + 1, LANES * t : LANES * (t + 1)]
+
+        return jnp.where(is_right, row_of(t + 1), row_of(t - 1)) if beyond else row_of(t)
+
+    def fill(t, beyond, low, high):
+        band = lax.broadcasted_iota(jnp.int32, (high - low, LANES), 0) + low
+        shift = LANES if beyond else 0
+        masks = [
+            band == jnp.bitwise_and(lane + shift + off_row(k, t, beyond), 2 * LANES - 1) for k in range(links)
+        ]
+        at = 2 * shift
+        for h in range(hl):
+            d_real, d_imag = adm_row(0, 0, h, t, beyond), adm_row(1, 0, h, t, beyond)
+            total_real = jnp.zeros(band.shape, jnp.float32)
+            total_imag = jnp.zeros(band.shape, jnp.float32)
+            for k in range(links):
+                l_real, l_imag = adm_row(0, 1 + k, h, t, beyond), adm_row(1, 1 + k, h, t, beyond)
+                total_real += jnp.where(masks[k], d_real * l_real - d_imag * l_imag, 0.0)
+                total_imag += jnp.where(masks[k], d_real * l_imag + d_imag * l_real, 0.0)
+            weights[h, t, low:high, at : at + LANES] = total_real.astype(jnp.bfloat16)
+            weights[h, t, low:high, at + LANES : at + 2 * LANES] = total_imag.astype(jnp.bfloat16)
+
+    for t in range(tiles):
+        fill(t, False, 0, LANES + 16)
+        fill(t, False, 2 * LANES - 16, 2 * LANES)
+        for h in range(hl):
+            weights[h, t, LANES + 16 : 2 * LANES - 16, :] = jnp.zeros((LANES - 32, 4 * LANES), jnp.bfloat16)
+            weights[h, t, 16 : LANES - 16, 2 * LANES :] = jnp.zeros((LANES - 32, 2 * LANES), jnp.bfloat16)
+
+    pl.semaphore_wait(barrier, nh - 1 + nh * has_left.astype(jnp.int32) + nh * has_right.astype(jnp.int32))
+
+    def remote(src, dst, send_sem, recv_sem, d, by):
+        return pltpu.make_async_remote_copy(
+            src_ref=src, dst_ref=dst, send_sem=send_sem, recv_sem=recv_sem, device_id={"harm": d, "bus": by}
+        )
+
+    def bus_copy(d, slot, by, sems):
+        return remote(my_bus, buses.at[slot], sems.at[d], bus_recv.at[slot], d, by)
+
+    def spec_copy(d, slot, by, sems):
+        return remote(send.at[d], recv.at[slot], sems.at[d], spec_recv.at[slot], d, by)
+
+    def ret_copy(d, source):
+        place = next_ref.at[:, pl.ds(source * hl, hl)]
+        return remote(send_back.at[d], place, ret_send.at[d], ret_recv.at[source], d, y)
+
+    def side_copies(side):
+        by = y + 1 if side == 0 else y - 1
+        start = block - LANES if side == 0 else 0
+        return (
+            remote(
+                adm_ref.at[:, :, :, pl.ds(start, LANES)],
+                adm_side.at[side],
+                side_send.at[side],
+                side_recv.at[side],
+                me,
+                by,
+            ),
+            remote(
+                off_ref.at[:, pl.ds(start, LANES)],
+                off_side.at[side],
+                side_send.at[2 + side],
+                side_recv.at[2 + side],
+                me,
+                by,
+            ),
+        )
+
+    send_right = jnp.logical_and(has_right, me == nh - 1)
+    send_left = jnp.logical_and(has_left, me == 0)
+
+    def each(low, body):
+        def step(i, carry):
+            body(i)
+            return carry
+
+        lax.fori_loop(low, nh, step, 0)
+
+    def peer(s):
+        return lax.rem(me + s, nh)
+
+    each(1, lambda s: bus_copy(peer(s), me + 1, y, bus_send).start())
+
+    @pl.when(send_right)
+    def _():
+        each(0, lambda d: bus_copy(d, 0, y + 1, bus_right).start())
+
+    @pl.when(send_left)
+    def _():
+        each(0, lambda d: bus_copy(d, nh + 1, y - 1, bus_left).start())
+
+    @pl.when(has_right)
+    def _():
+        for copy in side_copies(0):
+            copy.start()
+
+    @pl.when(has_left)
+    def _():
+        for copy in side_copies(1):
+            copy.start()
+
     span = volt_ref.shape[0] // conv
     per = LANES // conv
     for b in range(span // per):
@@ -121,147 +262,6 @@
         mixed = jnp.dot(back_ref[...], stacked, preferred_element_type=jnp.float32)
         count = LANES // per_dev
         send[count * b : count * (b + 1)] = mixed.reshape(count, hl, 8, LANES).astype(jnp.bfloat16)
-
-    first = (y * nh + me) * sub
-    row8 = lax.broadcasted_iota(jnp.int32, (8, LANES), 0) % conv
-    numbers = jnp.zeros((8, LANES), jnp.float32)
-    for c in range(conv):
-        numbers = jnp.where(row8 == c, (bus_ref[c] - first).astype(jnp.float32), numbers)
-    my_bus[...] = numbers.astype(jnp.bfloat16)
-
-    @pl.when(jnp.logical_not(has_left))
-    def _():
-        recv[0] = jnp.zeros(recv.shape[1:], recv.dtype)
-        buses[0] = jnp.zeros(buses.shape[1:], buses.dtype)
-        adm_side[0] = jnp.zeros(adm_side.shape[1:], adm_side.dtype)
-        off_side[0] = jnp.zeros(off_side.shape[1:], off_side.dtype)
-
-    @pl.when(jnp.logical_not(has_right))
-    def _():
-        recv[nh + 1] = jnp.zeros(recv.shape[1:], recv.dtype)
-        buses[nh + 1] = jnp.zeros(buses.shape[1:], buses.dtype)
-        adm_side[1] = jnp.zeros(adm_side.shape[1:], adm_side.dtype)
-        off_side[1] = jnp.zeros(off_side.shape[1:], off_side.dtype)
-
-    lane = lax.broadcasted_iota(jnp.int32, (1, LANES), 1)
-    is_right = lane < LANES // 2
-
-    def adm_row(p, k, h, t, beyond):
-        def row_of(t):
-            if t < 0:
-                return adm_side[0, p, k, h : h + 1, :]
-            if t >= tiles:
-                return adm_side[1, p, k, h : h + 1, :]
-            return adm_ref[p, k, h : h + 1, LANES * t : LANES * (t + 1)]
-
-        return jnp.where(is_right, row_of(t + 1), row_of(t - 1)) if beyond else row_of(t)
-
-    def off_row(k, t, beyond):
-        def row_of(t):
-            if t < 0:
-                return off_side[0, k : k + 1, :]
-            if t >= tiles:
-                return off_side[1, k : k + 1, :]
-            return off_ref[k : k + 1, LANES * t : LANES * (t + 1)]
-
-        return jnp.where(is_right, row_of(t + 1), row_of(t - 1)) if beyond else row_of(t)
-
-    def fill(t, beyond, low, high):
-        band = lax.broadcasted_iota(jnp.int32, (high - low, LANES), 0) + low
-        shift = LANES if beyond else 0
-        masks = [
-            band == jnp.bitwise_and(lane + shift + off_row(k, t, beyond), 2 * LANES - 1) for k in range(links)
-        ]
-        at = 2 * shift
-        for h in range(hl):
-            d_real, d_imag = adm_row(0, 0, h, t, beyond), adm_row(1, 0, h, t, beyond)
-            total_real = jnp.zeros(band.shape, jnp.float32)
-            total_imag = jnp.zeros(band.shape, jnp.float32)
-            for k in range(links):
-                l_real, l_imag = adm_row(0, 1 + k, h, t, beyond), adm_row(1, 1 + k, h, t, beyond)
-                total_real += jnp.where(masks[k], d_real * l_real - d_imag * l_imag, 0.0)
-                total_imag += jnp.where(masks[k], d_real * l_imag + d_imag * l_real, 0.0)
-            weights[h, t, low:high, at : at + LANES] = total_real.astype(jnp.bfloat16)
-            weights[h, t, low:high, at + LANES : at + 2 * LANES] = total_imag.astype(jnp.bfloat16)
-
-    for t in range(tiles):
-        fill(t, False, 0, LANES + 16)
-        fill(t, False, 2 * LANES - 16, 2 * LANES)
-        for h in range(hl):
-            weights[h, t, LANES + 16 : 2 * LANES - 16, :] = jnp.zeros((LANES - 32, 4 * LANES), jnp.bfloat16)
-            weights[h, t, 16 : LANES - 16, 2 * LANES :] = jnp.zeros((LANES - 32, 2 * LANES), jnp.bfloat16)
-
-    pl.semaphore_wait(barrier, nh - 1 + nh * has_left.astype(jnp.int32) + nh * has_right.astype(jnp.int32))
-
-    def remote(src, dst, send_sem, recv_sem, d, by):
-        return pltpu.make_async_remote_copy(
-            src_ref=src, dst_ref=dst, send_sem=send_sem, recv_sem=recv_sem, device_id={"harm": d, "bus": by}
-        )
-
-    def bus_copy(d, slot, by, sems):
-        return remote(my_bus, buses.at[slot], sems.at[d], bus_recv.at[slot], d, by)
-
-    def spec_copy(d, slot, by, sems):
-        return remote(send.at[d], recv.at[slot], sems.at[d], spec_recv.at[slot], d, by)
-
-    def ret_copy(d, source):
-        place = next_ref.at[:, pl.ds(source * hl, hl)]
-        return remote(send_back.at[d], place, ret_send.at[d], ret_recv.at[source], d, y)
-
-    def side_copies(side):
-        by = y + 1 if side == 0 else y - 1
-        start = block - LANES if side == 0 else 0
-        return (
-            remote(
-                adm_ref.at[:, :, :, pl.ds(start, LANES)],
-                adm_side.at[side],
-                side_send.at[side],
-                side_recv.at[side],
-                me,
-                by,
-            ),
-            remote(
-                off_ref.at[:, pl.ds(start, LANES)],
-                off_side.at[side],
-                side_send.at[2 + side],
-                side_recv.at[2 + side],
-                me,
-                by,
-            ),
-        )
-
-    send_right = jnp.logical_and(has_right, me == nh - 1)
-    send_left = jnp.logical_and(has_left, me == 0)
-
-    def each(low, body):
-        def step(i, carry):
-            body(i)
-            return carry
-
-        lax.fori_loop(low, nh, step, 0)
-
-    def peer(s):
-        return lax.rem(me + s, nh)
-
-    each(1, lambda s: bus_copy(peer(s), me + 1, y, bus_send).start())
-
-    @pl.when(send_right)
-    def _():
-        each(0, lambda d: bus_copy(d, 0, y + 1, bus_right).start())
-
-    @pl.when(send_left)
-    def _():
-        each(0, lambda d: bus_copy(d, nh + 1, y - 1, bus_left).start())
-
-    @pl.when(has_right)
-    def _():
-        for copy in side_copies(0):
-            copy.start()
-
-    @pl.when(has_left)
-    def _():
-        for copy in side_copies(1):
-            copy.start()
 
     each(1, lambda s: spec_copy(peer(s), me + 1, y, spec_send).start())
 

time: 24.1 us -> 23.7 us (0.983)
  Pallas kernels: 23.3 us -> 22.9 us
    pallas_call x1, Pallas kernels: 22.5 us -> 22 us  [local(): pl.pallas_call(functools.partial(kernel, nh, ny), out_shape=(pltpu.VMEM(v...]
where the time goes in v4:
time: 23.7 us; the launch traced here: 23.5 us
  Pallas kernels  22.9 us (97%)
  between operations  0.64 us (3%)
    pallas_call x1, Pallas kernels, local(): pl.pallas_call(functools.partial(kernel, nh, ny), out_shape=(pltpu.VMEM(v...  22 us
    pallas_call x1, Pallas kernels, local(): pl.pallas_call(store, out_shape=(jax.ShapeDtypeStruct(volt_shape, bf16),...  0.86 us

profile of v4, /device:TPU:0, one launch (start us, length us, event | category | flops | bytes accessed | tf_op | source)
XLA Modules:
  0.0 23.5 jit_solution(3851552196754448302)
XLA Ops:
  0.6 22.0 %power_flow.1 = (bf16[2,4,256,128]{3,2,1,0:T(8,128)(2,1)S(1)}, bf16[2,64,4,128]{3,2,1,0:T(4,128)(2,1)S(1)}) custom-call(bf16[512,128]{1,0:T(8,128)(2,1)} %bitcast.1, f32[4,128]{1,0:T(4,128)} %power_ref.1, s32[4]{0:T(128)} %type_ref.1, f32[8]{0:T(128)} %steep_ref.1, s32[4]{0:T(128)} %bus_ref.1, f32[2,4,4,256]{3,2,1,0:T(4,128)} %adm_ref.1, s32[3,256]{1,0:T(4,128)} %off_ref.1, ...), custom_call_target="tpu_custom_call" | custom-call | tf_op jit(solution)/shard_map/power_flow/pallas_call | solution.py:426
  22.7 0.9 %store_results.1 = (bf16[2,4,256,128]{3,2,1,0:T(8,128)(2,1)}, bf16[2,64,4,128]{3,2,1,0:T(4,128)(2,1)}) custom-call(bf16[2,4,256,128]{3,2,1,0:T(8,128)(2,1)S(1)} %get-tuple-element.4.volt_ref, bf16[2,64,4,128]{3,2,1,0:T(4,128)(2,1)S(1)} %get-tuple-element.5.next_ref), custom_call_target="tpu_custom_call" | custom-call | tf_op jit(solution)/shard_map/store_results/pallas_call | solution.py:471
